TPU v7x, 32 devices: a whole 2x2x4 slice. The times are simulated.
32 devices in a mesh: groups: 2 (over x), example: 8 (over z, y), cls: 2 (over core).
Axes of the slice: x: 2, y: 2, z: 4, core: 2. Of those that a mesh axis runs over, the one named last changes fastest.
Arguments:
- features: bfloat16 [2048, 4096], P(('groups', 'example'), 'cls'), parts along dimension 0
- weights: float32 [8192, 8192], P(('groups', 'cls'), 'example'), parts along dimension 0
- labels: int32 [2048], P(('groups', 'example')), parts along dimension 0, may hold values from 0 to 8191
- counts: int32 [16], P(('groups', 'example')), parts along dimension 0, may hold values from 16 to 128, as said below
- active: int32 [2], P('groups'), parts along dimension 0, may hold values from 4096 to 8192
Outputs:
- moved: float32 [8192, 8192], P(('groups', 'cls'), 'example'), parts along dimension 0
- losses: float32 [2048], P(('groups', 'example')), parts along dimension 0
There are 2 independent parts, one for each index of `groups`. A program takes and returns all parts, laid end to end along the dimension named above; each array names one. Nothing has to cross between parts.
Inputs may be any that keep to these rules, and one draw needn't show every extreme that they name: `counts`: each block has at least 16 valid slots; some block is full in every draw.
All inputs are finite; a program needn't handle non-finite values.
Results may differ from a plain program's by a relative error of at most 0.006.
Values may be sent and summed in bfloat16 or wider, within the bound.
A program may use at most 128 MiB of HBM per device.

v0:
```python
import jax
import jax.numpy as jnp
from jax import lax
from jax.sharding import PartitionSpec as P

FEATURES = 4096
CLASSES = 8192
ITERS = 2
NEGATIVE = -1e30
LEARNING_RATE = 2e-05
DAMPING_SHARE = 0.1
EPSILON = 1e-06


def body(features, weights, labels, counts, active):
    gathered, labels_all, counts_all = (
        lax.all_gather(features, "example", axis=0, tiled=True),
        lax.all_gather(labels, "example", axis=0, tiled=True),
        lax.all_gather(counts, "example", axis=0, tiled=True),
    )
    all_rows = gathered.shape[0]
    per_device = features.shape[0]
    local_classes = weights.shape[1]
    row_index = jnp.arange(all_rows)
    owner = row_index // per_device
    blocks = jnp.arange(counts_all.shape[0])
    row_limit = jnp.sum(
        jnp.where(owner[:, None] == blocks[None, :], counts_all[None, :], 0), axis=1
    )
    is_valid = (row_index % per_device < row_limit).astype(jnp.float32)
    valid_total = jnp.sum(counts_all).astype(jnp.float32)
    active_count = active[0]
    class_index = lax.axis_index("example") * local_classes + jnp.arange(local_classes)
    is_active = class_index < active_count
    target = (labels_all % active_count).astype(jnp.int32)
    squares = gathered * gathered
    current = weights
    moved = jnp.zeros_like(weights)
    denominator = None
    losses_all = None
    for iteration in range(ITERS):
        current_low = current.astype(jnp.bfloat16)
        logits = lax.psum_scatter(
            jnp.dot(gathered, current_low, preferred_element_type=jnp.float32),
            "cls",
            scatter_dimension=0,
            tiled=True,
        )
        row_start = lax.axis_index("cls") * logits.shape[0]
        row_number = logits.shape[0]
        row_valid = lax.dynamic_slice_in_dim(is_valid, row_start, row_number, 0)
        row_target = lax.dynamic_slice_in_dim(target, row_start, row_number, 0)
        is_label = class_index[None, :] == row_target[:, None]
        masked = jnp.where(is_active[None, :], logits, NEGATIVE)
        local_peak = jnp.max(masked, axis=1)
        local_label = jnp.sum(jnp.where(is_label, logits, 0.0), axis=1)
        row_peak = lax.pmax(local_peak, "example")
        exponent = jnp.exp(masked - row_peak[:, None])
        row_total, label_logit = lax.psum((jnp.sum(exponent, axis=1), local_label), "example")
        probability = exponent / row_total[:, None]
        residual = (
            row_valid[:, None] * (probability - is_label.astype(jnp.float32)) / valid_total
        ).astype(jnp.bfloat16)
        losses_all = row_valid * (row_peak + jnp.log(row_total) - label_logit)
        fisher_weight = None
        if iteration == 0:
            fisher_weight = (
                row_valid[:, None] * probability * (1.0 - probability) / valid_total
            ).astype(jnp.bfloat16)
        if iteration == 0:
            residual, fisher_weight, losses_all = (
                lax.all_gather(residual, "cls", axis=0, tiled=True),
                lax.all_gather(fisher_weight, "cls", axis=0, tiled=True),
                lax.all_gather(losses_all.astype(jnp.bfloat16), "cls", axis=0, tiled=True).astype(
                    losses_all.dtype
                ),
            )
        else:
            residual, losses_all = (
                lax.all_gather(residual, "cls", axis=0, tiled=True),
                lax.all_gather(losses_all.astype(jnp.bfloat16), "cls", axis=0, tiled=True).astype(
                    losses_all.dtype
                ),
            )
        gradient = lax.dot_general(
            gathered, residual, (((0,), (0,)), ((), ())), preferred_element_type=jnp.float32
        )
        if iteration == 0:
            fisher = lax.dot_general(
                squares, fisher_weight, (((0,), (0,)), ((), ())), preferred_element_type=jnp.float32
            )
            fisher_sum = lax.psum(jnp.sum(fisher), ("example", "cls"))
            damping = DAMPING_SHARE * fisher_sum / (FEATURES * CLASSES) + EPSILON
            denominator = fisher + damping
        change = gradient / denominator
        current = current - LEARNING_RATE * change
        moved = moved - change
    own_losses = lax.dynamic_slice_in_dim(
        losses_all, lax.axis_index("example") * per_device, per_device, 0
    )
    return (moved, own_losses)


def solution(mesh):
    return jax.shard_map(
        body,
        mesh=mesh,
        in_specs=(
            P(("groups", "example"), "cls"),
            P(("groups", "cls"), "example"),
            P(("groups", "example")),
            P(("groups", "example")),
            P("groups"),
        ),
        out_specs=(P(("groups", "cls"), "example"), P(("groups", "example"))),
        check_vma=False,
    )
```

profile of v0, /device:TPU:0, one launch (start us, length us, event | category | flops | bytes accessed | tf_op | source)
XLA Modules:
  0.0 353.1 jit_solution(9420997783361034570)
XLA Ops:
  7.9 77.7 %all-gather.7.cloned.1.call-done = bf16[1024,2048]{1,0:T(8,128)(2,1)} async-done(((bf16[128,2048]{1,0:T(8,128)(2,1)}), bf16[1024,2048]{1,0:T(8,128)(2,1)}) %all-gather.7.cloned.1.call-update) | async-done | bytes 4194320 | tf_op jit(solution)/shard_map/all_gather | solution.py:17
  85.6 11.2 %fusion.5 = f32[1024,1024]{1,0:T(8,128)} fusion(bf16[1024,2048]{1,0:T(8,128)(2,1)} %all-gather.7.cloned.1.call-done, f32[2048,1024]{1,0:T(8,128)} %param.6), kind=kOutput, calls=%fused_computation.8 | convolution fusion | flops 4297064448 | bytes 16777216 | tf_op jit(solution)/shard_map/dot_general | solution.py:44
  98.9 9.9 %all-reduce = s32[8]{0:T(128)S(1)} all-reduce(s32[8]{0:T(128)S(1)} %dynamic-update-slice), channel_id=1, replica_groups=mesh['groups'=2,'example'=8,'cls'=2] {'example'}, use_global_device_ids=true, to_apply=%add | all-reduce | flops 8 | bytes 64
  110.7 18.2 %all-gather = s32[8,1,128]{2,1,0:T(1,128)S(1)} all-gather(s32[1,1,128]{2,1,0:T(1,128)S(1)} %bitcast.28), channel_id=1, replica_groups=mesh['groups'=2,'example'=8,'cls'=2] {'example'}, dimensions={0}, use_global_device_ids=true | all-gather | bytes 4608 | tf_op jit(solution)/shard_map/all_gather | solution.py:18
  129.4 2.0 select_reduce_fusion.1
  131.4 17.2 %pmax.14 = f32[512]{0:T(512)S(1)} all-reduce(f32[512]{0:T(512)S(1)} %select_reduce_fusion.1), channel_id=1, replica_groups=mesh['groups'=2,'example'=8,'cls'=2] {'example'}, use_global_device_ids=true, to_apply=%region_3.4 | all-reduce | flops 512 | bytes 4096 | tf_op jit(solution)/shard_map/pmax | solution.py:57
  149.1 19.1 %psum.28 = f32[512]{0:T(512)S(1)} all-reduce(f32[512]{0:T(512)S(1)} %fusion.16), channel_id=1, replica_groups=mesh['groups'=2,'example'=8,'cls'=2] {'example'}, use_global_device_ids=true, to_apply=%region_5.6 | all-reduce | flops 512 | bytes 4096 | tf_op jit(solution)/shard_map/psum | solution.py:59
  168.1 2.8 fusion.13
  171.6 9.2 %copy.16 = f32[2048,1024]{0,1:T(8,128)} copy(f32[2048,1024]{1,0:T(8,128)} %param.6) | data formatting | bytes 16777216 | tf_op args[1]
  180.8 11.4 %fusion.26 = (f32[]{:T(128)}, f32[2048,1024]{1,0:T(8,128)}) fusion(bf16[1024,1024]{1,0:T(8,128)(2,1)} %all-gather.11.cloned.1.call-done, bf16[1024,2048]{1,0:T(8,128)(2,1)} %all-gather.7.cloned.1.call-done), kind=kOutput, calls=%fused_computation.49 | convolution fusion | flops 4299161600 | bytes 14680068 | tf_op jit(solution)/shard_map/dot_general | solution.py:89
  192.2 33.1 %psum.29 = f32[]{:T(128)} all-reduce(f32[]{:T(128)} %get-tuple-element.14), channel_id=1, replica_groups=mesh['groups'=2,'example'=8,'cls'=2] {'example','cls'}, use_global_device_ids=true, to_apply=%region_8.9 | all-reduce | flops 1 | bytes 8 | tf_op jit(solution)/shard_map/psum | solution.py:92
  225.4 9.1 %copy.15 = f32[2048,1024]{0,1:T(8,128)} copy(f32[2048,1024]{1,0:T(8,128)} %get-tuple-element.15) | data formatting | bytes 16777216 | tf_op jit(solution)/shard_map/dot_general | solution.py:89
  235.2 10.1 %bitcast_divide_fusion.1 = f32[2048,1024]{0,1:T(8,128)S(1)} fusion(f32[2048,1024]{0,1:T(8,128)} %copy.15, bf16[1024,1024]{1,0:T(8,128)(2,1)} %all-gather.9.cloned.1.call-done, bf16[1024,2048]{1,0:T(8,128)(2,1)} %all-gather.7.cloned.1.call-done, f32[]{:T(128)S(6)} %add.68), kind=kOutput, calls=%fused_computation.2 | convolution fusion | flops 4299161600 | bytes 23068676 | tf_op jit(solution)/shard_map/dot_general | solution.py:85
  245.3 3.4 copy-done.5
  248.7 9.5 %fusion.7 = f32[1024,1024]{1,0:T(8,128)} fusion(bf16[1024,2048]{1,0:T(8,128)(2,1)S(1)} %copy-done.3, f32[2048,1024]{0,1:T(8,128)} %copy.16, f32[2048,1024]{0,1:T(8,128)S(1)} %bitcast_divide_fusion.1), kind=kOutput, calls=%fused_computation.13 | convolution fusion | flops 4301258752 | bytes 25165824 | tf_op jit(solution)/shard_map/dot_general | solution.py:44
  258.3 9.4 %reduce-scatter.5.cloned.1.call-done = f32[512,1024]{1,0:T(8,128)} async-done(((f32[1024,1024]{1,0:T(8,128)}), f32[512,1024]{1,0:T(8,128)}) %reduce-scatter.5.cloned.1.call-update) | async-done | bytes 2097168 | tf_op jit(solution)/shard_map/reduce_scatter | solution.py:43
  267.7 2.0 select_reduce_fusion
  269.7 21.7 %pmax.15 = f32[512]{0:T(512)S(1)} all-reduce(f32[512]{0:T(512)S(1)} %select_reduce_fusion), channel_id=1, replica_groups=mesh['groups'=2,'example'=8,'cls'=2] {'example'}, use_global_device_ids=true, to_apply=%region_11.12 | all-reduce | flops 512 | bytes 4096 | tf_op jit(solution)/shard_map/pmax | solution.py:57
  292.2 17.2 %all-reduce.1 = (f32[512]{0:T(512)S(1)}, f32[512]{0:T(512)S(1)}) all-reduce(f32[512]{0:T(512)S(1)} %get-tuple-element.9, f32[512]{0:T(512)S(1)} %get-tuple-element.8), channel_id=1, replica_groups=mesh['groups'=2,'example'=8,'cls'=2] {'example'}, use_global_device_ids=true, to_apply=%region_13.14 | all-reduce | flops 1024 | bytes 8192 | tf_op jit(solution)/shard_map/psum | solution.py:59
  309.3 2.1 fusion.14
  311.6 2.0 all-gather.1
  314.2 6.6 %all-gather.13.cloned.1.call-done = bf16[1024,1024]{1,0:T(8,128)(2,1)} async-done(((bf16[512,1024]{1,0:T(8,128)(2,1)}), bf16[1024,1024]{1,0:T(8,128)(2,1)}) %all-gather.13.cloned.1.call-update) | async-done | bytes 2097168 | tf_op jit(solution)/shard_map/all_gather | solution.py:80
  320.9 16.2 %fusion = f32[2048,1024]{0,1:T(8,128)} fusion(f32[2048,1024]{0,1:T(8,128)} %copy-done.5, f32[2048,1024]{0,1:T(8,128)} %copy.15, bf16[1024,1024]{1,0:T(8,128)(2,1)} %all-gather.13.cloned.1.call-done, bf16[1024,2048]{1,0:T(8,128)(2,1)} %all-gather.7.cloned.1.call-done, f32[]{:T(128)S(6)} %add.68), kind=kOutput, calls=%fused_computation.1 | convolution fusion | flops 4303355904 | bytes 31457284 | tf_op jit(solution)/shard_map/dot_general | solution.py:85
  337.1 9.2 %copy.18 = f32[2048,1024]{1,0:T(8,128)} copy(f32[2048,1024]{0,1:T(8,128)} %fusion) | data formatting | bytes 16777216
  (45 shorter events, 5.9 us)
Async XLA Ops:
  7.2 78.5 %all-gather.7.cloned.1.call-start = ((), (), s32[]{:S(2)}) async-start(), calls=%async_computation.2 | async-start | bytes 4718592 | tf_op jit(solution)/shard_map/all_gather | solution.py:17
  7.9 121.5 %reduce-scatter.3.cloned.1.call-start = ((), (), s32[]{:S(2)}) async-start(), calls=%async_computation.3 | async-start | bytes 6291456 | tf_op jit(solution)/shard_map/reduce_scatter | solution.py:43
  96.8 0.7 copy-start.4
  96.8 13.9 %copy-start.2 = (s32[128]{0:T(128)S(1)}, s32[128]{0:T(128)}, u32[]{:S(2)}) copy-start(s32[128]{0:T(128)} %param.7) | copy-start | bytes 1540
  96.8 84.0 %all-gather.11.cloned.1.call-start = ((), (), s32[]{:S(2)}) async-start(), calls=%async_computation.5 | async-start | bytes 3145728 | tf_op jit(solution)/shard_map/all_gather | solution.py:73
  129.4 19.2 %copy-start = (f32[512,1024]{1,0:T(8,128)S(1)}, f32[512,1024]{1,0:T(8,128)}, u32[]{:S(2)}) copy-start(f32[512,1024]{1,0:T(8,128)} %reduce-scatter.3.cloned.1.call-done) | copy-start | bytes 6291460
  170.9 64.2 %all-gather.9.cloned.1.call-start = ((), (), s32[]{:S(2)}) async-start(), calls=%async_computation.4 | async-start | bytes 3145728 | tf_op jit(solution)/shard_map/all_gather | solution.py:72
  171.5 96.2 %reduce-scatter.5.cloned.1.call-start = ((), (), s32[]{:S(2)}) async-start(), calls=%async_computation.6 | async-start | bytes 6291456 | tf_op jit(solution)/shard_map/reduce_scatter | solution.py:43
  235.2 13.5 %copy-start.3 = (bf16[1024,2048]{1,0:T(8,128)(2,1)S(1)}, bf16[1024,2048]{1,0:T(8,128)(2,1)}, u32[]{:S(2)}) copy-start(bf16[1024,2048]{1,0:T(8,128)(2,1)} %all-gather.7.cloned.1.call-done) | copy-start | bytes 12582916
  245.3 3.4 copy-start.5
  258.3 62.6 %all-gather.13.cloned.1.call-start = ((), (), s32[]{:S(2)}) async-start(), calls=%async_computation.7 | async-start | bytes 3145728 | tf_op jit(solution)/shard_map/all_gather | solution.py:80
  267.7 23.7 %copy-start.1 = (f32[512,1024]{1,0:T(8,128)S(1)}, f32[512,1024]{1,0:T(8,128)}, u32[]{:S(2)}) copy-start(f32[512,1024]{1,0:T(8,128)} %reduce-scatter.5.cloned.1.call-done) | copy-start | bytes 6291460
Sparse Core Ops, SparseCore 0:
  10.1 75.5 all-gather.6
  97.0 10.5 reduce-scatter.2
  171.1 7.7 all-gather.10
  180.3 11.7 all-gather.8
  258.4 9.2 reduce-scatter.4
  311.6 9.2 all-gather.12
where the time goes:
time: 354 us; the launch traced here: 353 us
  blocking collectives  138 us (39%)
  waiting for transfers between devices  95 us (27%)
  matrix products  58.4 us (16%)
  local copies, waits for them, and re-layouts  33.1 us (9%)
  between operations  16.8 us (5%)
  other arithmetic  11.1 us (3%)
    all_gather x1, waiting for transfers between devices, body(): lax.all_gather(features, 'example', axis=0, tiled=True)  77.7 us
    pmax x2, blocking collectives, body(): row_peak = lax.pmax(local_peak, 'example')  38.9 us
    psum x2, blocking collectives, body(): lax.psum((jnp.sum(exponent, axis=1), local_label), 'example')  36.3 us
    psum x1, blocking collectives, body(): fisher_sum = lax.psum(jnp.sum(fisher), ('example', 'cls'))  33.1 us
    dot_general x2, matrix products, body(): lax.dot_general(gathered, residual, (((0,), (0,)), ((), ())), preferred_e...  26.3 us
    unnamed x18, local copies, waits for them, and re-layouts  23.2 us
    dot_general x2, matrix products, body(): jnp.dot(gathered, current_low, preferred_element_type=jnp.float32)  20.7 us
    all_gather x1, blocking collectives, body(): lax.all_gather(labels, 'example', axis=0, tiled=True)  18.2 us
  transfers between devices with their start and end apart: 6, of which 3 were waited for; matrix products, arithmetic and copies ran while one was open for 9% of the time, Pallas kernels for 0%

commit v1 on v0

--- a/solution.py
+++ b/solution.py
@@ -12,9 +12,31 @@
 EPSILON = 1e-06
 
 
+def joined_along(blocks, dim):
+    blocks = jnp.moveaxis(blocks, 0, dim)
+    dims = blocks.shape
+    return blocks.reshape(*dims[:dim], dims[dim] * dims[dim + 1], *dims[dim + 2 :])
+
+
+def ring_gather(shard, axis, dim):
+    size = lax.axis_size(axis)
+    pairs = [(i, (i + 1) % size) for i in range(size)]
+    back = [(b, a) for a, b in pairs]
+    lower, upper = ([], [])
+    for lap in range(size - 1):
+        if lap % 2 == 0:
+            lower.append(lax.ppermute(lower[-1] if lower else shard, axis, pairs))
+        else:
+            upper.append(lax.ppermute(upper[-1] if upper else shard, axis, back))
+    parts = jnp.stack([*lower[::-1], shard, *upper])
+    shift = lax.axis_index(axis) - len(lower)
+    parts = parts[(jnp.arange(size) - shift) % size]
+    return joined_along(parts, dim)
+
+
 def body(features, weights, labels, counts, active):
     gathered, labels_all, counts_all = (
-        lax.all_gather(features, "example", axis=0, tiled=True),
+        ring_gather(features, "example", 0),
         lax.all_gather(labels, "example", axis=0, tiled=True),
         lax.all_gather(counts, "example", axis=0, tiled=True),
     )

time: 354 us -> 362 us (1.023)
  starting transfers between devices: 0.24 us -> 39.2 us
  waiting for transfers between devices: 95 us -> 72.7 us
  local copies, waits for them, and re-layouts: 33.1 us -> 18 us
  blocking collectives: 138 us -> 142 us
    all_gather x1 -> x0, waiting for transfers between devices: 77.7 us -> none  [body(): lax.all_gather(features, 'example', axis=0, tiled=True)]
    ppermute x0 -> x7, waiting for transfers between devices: none -> 49.5 us  [the longest x4 49.5 us: ring_gather(): lower.append(lax.ppermute(lower[-1] if lower else shard, axis, pairs))]
    ppermute x0 -> x7, starting transfers between devices: none -> 38.6 us  [the longest x3 30.6 us: ring_gather(): upper.append(lax.ppermute(upper[-1] if upper else shard, axis, back))]
    unnamed x18 -> x25, local copies, waits for them, and re-layouts: 23.2 us -> 11.4 us
    dot_general x1 -> x0, local copies, waits for them, and re-layouts: 9.14 us -> none  [body(): lax.dot_general(squares, fisher_weight, (((0,), (0,)), ((), ())), preferr...]
    all_gather x1, waiting for transfers between devices: 0.01 us -> 6.36 us  [body(): lax.all_gather(fisher_weight, 'cls', axis=0, tiled=True)]
    gather x0 -> x1, local copies, waits for them, and re-layouts: none -> 4.98 us  [ring_gather(): parts = parts[(jnp.arange(size) - shift) % size]]
    all_gather x1, blocking collectives: 18.2 us -> 22.7 us  [body(): lax.all_gather(labels, 'example', axis=0, tiled=True)]
  transfers between devices with their start and end apart: 6 -> 12, of which waited for: 3 -> 7; matrix products, arithmetic and copies ran while one was open for 9% -> 6% of each run, Pallas kernels for 0% -> 0%
where the time goes in v1:
time: 362 us; the launch traced here: 361 us
  blocking collectives  142 us (39%)
  waiting for transfers between devices  72.7 us (20%)
  matrix products  58.7 us (16%)
  starting transfers between devices  39.2 us (11%)
  local copies, waits for them, and re-layouts  18 us (5%)
  between operations  16.5 us (5%)
  other arithmetic  14.3 us (4%)
    ppermute x4, waiting for transfers between devices, ring_gather(): lower.append(lax.ppermute(lower[-1] if lower else shard, axis, pairs))  49.5 us
    pmax x2, blocking collectives, body(): row_peak = lax.pmax(local_peak, 'example')  38.9 us
    psum x2, blocking collectives, body(): lax.psum((jnp.sum(exponent, axis=1), local_label), 'example')  36.3 us
    psum x1, blocking collectives, body(): fisher_sum = lax.psum(jnp.sum(fisher), ('example', 'cls'))  34.5 us
    ppermute x3, starting transfers between devices, ring_gather(): upper.append(lax.ppermute(upper[-1] if upper else shard, axis, back))  30.6 us
    dot_general x2, matrix products, body(): lax.dot_general(gathered, residual, (((0,), (0,)), ((), ())), preferred_e...  26.5 us
    all_gather x1, blocking collectives, body(): lax.all_gather(labels, 'example', axis=0, tiled=True)  22.7 us
    dot_general x2, matrix products, body(): jnp.dot(gathered, current_low, preferred_element_type=jnp.float32)  20.6 us
  transfers between devices with their start and end apart: 12, of which 7 were waited for; matrix products, arithmetic and copies ran while one was open for 6% of the time, Pallas kernels for 0%

profile of v1, /device:TPU:0, one launch (start us, length us, event | category | flops | bytes accessed | tf_op | source)
XLA Modules:
  0.0 361.0 jit_solution(9159252250459676846)
XLA Ops:
  10.3 15.2 %collective-permute-done = bf16[128,2048]{1,0:T(8,128)(2,1)S(1)} collective-permute-done((bf16[128,2048]{1,0:T(8,128)(2,1)}, bf16[128,2048]{1,0:T(8,128)(2,1)S(1)}, u32[]{:S(2)}, u32[]{:S(2)}) %collective-permute-start) | collective-permute-done | bytes 524320 | tf_op jit(solution)/shard_map/ppermute | solution.py:28
  25.4 4.7 %collective-permute-start.4 = (bf16[128,2048]{1,0:T(8,128)(2,1)}, bf16[128,2048]{1,0:T(8,128)(2,1)S(1)}, u32[]{:S(2)}, u32[]{:S(2)}) collective-permute-start(bf16[128,2048]{1,0:T(8,128)(2,1)} %param.5), channel_id=1, source_target_pairs={{2,0},{4,2},{6,4},{8,6},{10,8},{12,10},{14,12},{0,14},{3,1},{5,3},... | collective-permute-start | bytes 1572872 | tf_op jit(solution)/shard_map/ppermute | solution.py:30
  30.2 17.4 %collective-permute-done.1 = bf16[128,2048]{1,0:T(8,128)(2,1)S(1)} collective-permute-done((bf16[128,2048]{1,0:T(8,128)(2,1)S(1)}, bf16[128,2048]{1,0:T(8,128)(2,1)S(1)}, u32[]{:S(2)}, u32[]{:S(2)}) %collective-permute-start.1) | collective-permute-done | bytes 524320 | tf_op jit(solution)/shard_map/ppermute | solution.py:28
  50.0 12.3 %collective-permute-start.5 = (bf16[128,2048]{1,0:T(8,128)(2,1)S(1)}, bf16[128,2048]{1,0:T(8,128)(2,1)S(1)}, u32[]{:S(2)}, u32[]{:S(2)}) collective-permute-start(bf16[128,2048]{1,0:T(8,128)(2,1)S(1)} %collective-permute-done.4), channel_id=1, source_target_pairs={{2,0},{4,2},{6,4},{8,6},{10,8},{12,10},{14,12},{0,14},{3,1},{5,3},... | collective-permute-start | bytes 1572872 | tf_op jit(solution)/shard_map/ppermute | solution.py:30
  62.4 8.9 %collective-permute-done.2 = bf16[128,2048]{1,0:T(8,128)(2,1)S(1)} collective-permute-done((bf16[128,2048]{1,0:T(8,128)(2,1)S(1)}, bf16[128,2048]{1,0:T(8,128)(2,1)S(1)}, u32[]{:S(2)}, u32[]{:S(2)}) %collective-permute-start.2) | collective-permute-done | bytes 524320 | tf_op jit(solution)/shard_map/ppermute | solution.py:28
  73.8 13.5 %collective-permute-start.6 = (bf16[128,2048]{1,0:T(8,128)(2,1)S(1)}, bf16[128,2048]{1,0:T(8,128)(2,1)S(1)}, u32[]{:S(2)}, u32[]{:S(2)}) collective-permute-start(bf16[128,2048]{1,0:T(8,128)(2,1)S(1)} %collective-permute-done.5), channel_id=1, source_target_pairs={{2,0},{4,2},{6,4},{8,6},{10,8},{12,10},{14,12},{0,14},{3,1},{5,3},... | collective-permute-start | bytes 1572872 | tf_op jit(solution)/shard_map/ppermute | solution.py:30
  87.4 8.0 %collective-permute-done.3 = bf16[128,2048]{1,0:T(8,128)(2,1)} collective-permute-done((bf16[128,2048]{1,0:T(8,128)(2,1)S(1)}, bf16[128,2048]{1,0:T(8,128)(2,1)}, u32[]{:S(2)}, u32[]{:S(2)}) %collective-permute-start.3) | collective-permute-done | bytes 524320 | tf_op jit(solution)/shard_map/ppermute | solution.py:28
  103.1 5.0 %gather_fusion = bf16[8,128,2048]{2,1,0:T(8,128)(2,1)} fusion(bf16[8,128,2048]{2,1,0:T(8,128)(2,1)} %bitcast_dynamic-update-slice_fusion, s32[1024]{0:T(1024)S(1)} %pad_clamp_fusion), kind=kCustom, calls=%fused_computation | custom fusion | bytes 8388640 | tf_op jit(solution)/shard_map/gather | solution.py:33
  108.0 11.2 %fusion.4 = f32[1024,1024]{1,0:T(8,128)} fusion(bf16[1024,2048]{1,0:T(8,128)(2,1)} %bitcast.36, f32[2048,1024]{1,0:T(8,128)} %param.6), kind=kOutput, calls=%fused_computation.8 | convolution fusion | flops 4297064448 | bytes 16777216 | tf_op jit(solution)/shard_map/dot_general | solution.py:66
  121.3 7.4 %all-reduce = s32[8]{0:T(128)S(1)} all-reduce(s32[8]{0:T(128)S(1)} %dynamic-update-slice), channel_id=1, replica_groups=mesh['groups'=2,'example'=8,'cls'=2] {'example'}, use_global_device_ids=true, to_apply=%add | all-reduce | flops 8 | bytes 64
  130.6 22.7 %all-gather = s32[8,1,128]{2,1,0:T(1,128)S(1)} all-gather(s32[1,1,128]{2,1,0:T(1,128)S(1)} %bitcast.44), channel_id=1, replica_groups=mesh['groups'=2,'example'=8,'cls'=2] {'example'}, dimensions={0}, use_global_device_ids=true | all-gather | bytes 4608 | tf_op jit(solution)/shard_map/all_gather | solution.py:40
  155.8 17.1 %pmax.14 = f32[512]{0:T(512)S(1)} all-reduce(f32[512]{0:T(512)S(1)} %select_reduce_fusion.1), channel_id=1, replica_groups=mesh['groups'=2,'example'=8,'cls'=2] {'example'}, use_global_device_ids=true, to_apply=%region_3.4 | all-reduce | flops 512 | bytes 4096 | tf_op jit(solution)/shard_map/pmax | solution.py:79
  175.0 19.1 %psum.28 = f32[512]{0:T(512)S(1)} all-reduce(f32[512]{0:T(512)S(1)} %fusion.14), channel_id=1, replica_groups=mesh['groups'=2,'example'=8,'cls'=2] {'example'}, use_global_device_ids=true, to_apply=%region_5.6 | all-reduce | flops 512 | bytes 4096 | tf_op jit(solution)/shard_map/psum | solution.py:81
  197.9 6.4 %all-gather.8.cloned.1.call-done = bf16[1024,1024]{1,0:T(8,128)(2,1)} async-done(((bf16[512,1024]{1,0:T(8,128)(2,1)}), bf16[1024,1024]{1,0:T(8,128)(2,1)}) %all-gather.8.cloned.1.call-update) | async-done | bytes 2097168 | tf_op jit(solution)/shard_map/all_gather | solution.py:95
  204.3 11.7 %fusion.26 = (f32[]{:T(128)}, f32[2048,1024]{1,0:T(8,128)}) fusion(bf16[1024,1024]{1,0:T(8,128)(2,1)} %all-gather.8.cloned.1.call-done, bf16[1024,2048]{1,0:T(8,128)(2,1)} %bitcast.37), kind=kOutput, calls=%fused_computation.63 | convolution fusion | flops 4299161600 | bytes 14680068 | tf_op jit(solution)/shard_map/dot_general | solution.py:111
  215.9 34.5 %psum.29 = f32[]{:T(128)} all-reduce(f32[]{:T(128)} %get-tuple-element.8), channel_id=1, replica_groups=mesh['groups'=2,'example'=8,'cls'=2] {'example','cls'}, use_global_device_ids=true, to_apply=%region_8.9 | all-reduce | flops 1 | bytes 8 | tf_op jit(solution)/shard_map/psum | solution.py:114
  251.1 10.1 %add_divide_fusion = f32[2048,1024]{1,0:T(8,128)S(1)} fusion(f32[2048,1024]{1,0:T(8,128)} %get-tuple-element.9, f32[]{:T(128)S(6)} %add.94, bf16[1024,2048]{1,0:T(8,128)(2,1)} %bitcast.38, bf16[1024,1024]{1,0:T(8,128)(2,1)} %all-gather.6.cloned.1.call-done), kind=kOutput, calls=%fused_computation.3 | convolution fusion | flops 4299161600 | bytes 23068676 | tf_op jit(solution)/shard_map/dot_general | solution.py:107
  261.3 3.2 copy-done.6
  264.5 9.4 %fusion = f32[1024,1024]{1,0:T(8,128)} fusion(bf16[1024,2048]{1,0:T(8,128)(2,1)S(1)} %bitcast.40, f32[2048,1024]{1,0:T(8,128)} %param.6, f32[2048,1024]{1,0:T(8,128)S(1)} %add_divide_fusion), kind=kOutput, calls=%fused_computation.4 | convolution fusion | flops 4301258752 | bytes 25165824 | tf_op jit(solution)/shard_map/dot_general | solution.py:66
  274.2 9.2 %reduce-scatter.5.cloned.1.call-done = f32[512,1024]{1,0:T(8,128)} async-done(((f32[1024,1024]{1,0:T(8,128)}), f32[512,1024]{1,0:T(8,128)}) %reduce-scatter.5.cloned.1.call-update) | async-done | bytes 2097168 | tf_op jit(solution)/shard_map/reduce_scatter | solution.py:65
  285.4 21.8 %pmax.15 = f32[512]{0:T(512)S(1)} all-reduce(f32[512]{0:T(512)S(1)} %select_reduce_fusion), channel_id=1, replica_groups=mesh['groups'=2,'example'=8,'cls'=2] {'example'}, use_global_device_ids=true, to_apply=%region_11.12 | all-reduce | flops 512 | bytes 4096 | tf_op jit(solution)/shard_map/pmax | solution.py:79
  309.4 17.2 %all-reduce.1 = (f32[512]{0:T(512)S(1)}, f32[512]{0:T(512)S(1)}) all-reduce(f32[512]{0:T(512)S(1)} %get-tuple-element.3, f32[512]{0:T(512)S(1)} %get-tuple-element.2), channel_id=1, replica_groups=mesh['groups'=2,'example'=8,'cls'=2] {'example'}, use_global_device_ids=true, to_apply=%region_13.14 | all-reduce | flops 1024 | bytes 8192 | tf_op jit(solution)/shard_map/psum | solution.py:81
  331.3 6.9 %all-gather.10.cloned.1.call-done = bf16[1024,1024]{1,0:T(8,128)(2,1)} async-done(((bf16[512,1024]{1,0:T(8,128)(2,1)}), bf16[1024,1024]{1,0:T(8,128)(2,1)}) %all-gather.10.cloned.1.call-update) | async-done | bytes 2097168 | tf_op jit(solution)/shard_map/all_gather | solution.py:102
  338.1 16.4 %divide_subtract_fusion = f32[2048,1024]{1,0:T(8,128)} fusion(f32[2048,1024]{1,0:T(8,128)} %copy-done.6, f32[2048,1024]{1,0:T(8,128)} %get-tuple-element.9, f32[]{:T(128)S(6)} %add.94, bf16[1024,2048]{1,0:T(8,128)(2,1)} %bitcast.39, bf16[1024,1024]{1,0:T(8,128)(2,1)} %all-gather.10.cloned.1.call-done), kind=kOutput, calls=%fused_computation.1 | convolution fusion | flops 4303355904 | bytes 31457284 | tf_op jit(solution)/shard_map/dot_general | solution.py:107
  (66 shorter events, 35.3 us)
Async XLA Ops:
  7.2 92.6 %copy-start.3 = (bf16[128,2048]{1,0:T(8,128)(2,1)S(1)}, bf16[128,2048]{1,0:T(8,128)(2,1)}, u32[]{:S(2)}) copy-start(bf16[128,2048]{1,0:T(8,128)(2,1)} %param.5) | copy-start | bytes 1572868
  7.2 146.6 %reduce-scatter.3.cloned.1.call-start = ((), (), s32[]{:S(2)}) async-start(), calls=%async_computation.2 | async-start | bytes 6291456 | tf_op jit(solution)/shard_map/reduce_scatter | solution.py:65
  7.2 18.2 %collective-permute-start = (bf16[128,2048]{1,0:T(8,128)(2,1)}, bf16[128,2048]{1,0:T(8,128)(2,1)S(1)}, u32[]{:S(2)}, u32[]{:S(2)}) collective-permute-start(bf16[128,2048]{1,0:T(8,128)(2,1)} %param.5), channel_id=1, source_target_pairs={{0,2},{2,4},{4,6},{6,8},{8,10},{10,12},{12,14},{14,0},{1,3},{3,5},... | collective-permute-start | bytes 1572872 | tf_op jit(solution)/shard_map/ppermute | solution.py:28
  25.4 22.1 %collective-permute-start.1 = (bf16[128,2048]{1,0:T(8,128)(2,1)S(1)}, bf16[128,2048]{1,0:T(8,128)(2,1)S(1)}, u32[]{:S(2)}, u32[]{:S(2)}) collective-permute-start(bf16[128,2048]{1,0:T(8,128)(2,1)S(1)} %collective-permute-done), channel_id=1, source_target_pairs={{0,2},{2,4},{4,6},{6,8},{8,10},{10,12},{12,14},{14,0},{1,3},{3,5},... | collective-permute-start | bytes 1572872 | tf_op jit(solution)/shard_map/ppermute | solution.py:28
  25.4 24.6 %collective-permute-start.4 = (bf16[128,2048]{1,0:T(8,128)(2,1)}, bf16[128,2048]{1,0:T(8,128)(2,1)S(1)}, u32[]{:S(2)}, u32[]{:S(2)}) collective-permute-start(bf16[128,2048]{1,0:T(8,128)(2,1)} %param.5), channel_id=1, source_target_pairs={{2,0},{4,2},{6,4},{8,6},{10,8},{12,10},{14,12},{0,14},{3,1},{5,3},... | collective-permute-start | bytes 1572872 | tf_op jit(solution)/shard_map/ppermute | solution.py:30
  47.6 23.8 %collective-permute-start.2 = (bf16[128,2048]{1,0:T(8,128)(2,1)S(1)}, bf16[128,2048]{1,0:T(8,128)(2,1)S(1)}, u32[]{:S(2)}, u32[]{:S(2)}) collective-permute-start(bf16[128,2048]{1,0:T(8,128)(2,1)S(1)} %collective-permute-done.1), channel_id=1, source_target_pairs={{0,2},{2,4},{4,6},{6,8},{8,10},{10,12},{12,14},{14,0},{1,3},{3,5},... | collective-permute-start | bytes 1572872 | tf_op jit(solution)/shard_map/ppermute | solution.py:28
  50.0 23.8 %collective-permute-start.5 = (bf16[128,2048]{1,0:T(8,128)(2,1)S(1)}, bf16[128,2048]{1,0:T(8,128)(2,1)S(1)}, u32[]{:S(2)}, u32[]{:S(2)}) collective-permute-start(bf16[128,2048]{1,0:T(8,128)(2,1)S(1)} %collective-permute-done.4), channel_id=1, source_target_pairs={{2,0},{4,2},{6,4},{8,6},{10,8},{12,10},{14,12},{0,14},{3,1},{5,3},... | collective-permute-start | bytes 1572872 | tf_op jit(solution)/shard_map/ppermute | solution.py:30
  71.3 24.0 %collective-permute-start.3 = (bf16[128,2048]{1,0:T(8,128)(2,1)S(1)}, bf16[128,2048]{1,0:T(8,128)(2,1)}, u32[]{:S(2)}, u32[]{:S(2)}) collective-permute-start(bf16[128,2048]{1,0:T(8,128)(2,1)S(1)} %collective-permute-done.2), channel_id=1, source_target_pairs={{0,2},{2,4},{4,6},{6,8},{8,10},{10,12},{12,14},{14,0},{1,3},{3,5},... | collective-permute-start | bytes 1572872 | tf_op jit(solution)/shard_map/ppermute | solution.py:28
  73.8 28.4 %collective-permute-start.6 = (bf16[128,2048]{1,0:T(8,128)(2,1)S(1)}, bf16[128,2048]{1,0:T(8,128)(2,1)S(1)}, u32[]{:S(2)}, u32[]{:S(2)}) collective-permute-start(bf16[128,2048]{1,0:T(8,128)(2,1)S(1)} %collective-permute-done.5), channel_id=1, source_target_pairs={{2,0},{4,2},{6,4},{8,6},{10,8},{12,10},{14,12},{0,14},{3,1},{5,3},... | collective-permute-start | bytes 1572872 | tf_op jit(solution)/shard_map/ppermute | solution.py:30
  119.2 0.7 copy-start.5
  119.2 11.4 %copy-start.4 = (s32[128]{0:T(128)S(1)}, s32[128]{0:T(128)}, u32[]{:S(2)}) copy-start(s32[128]{0:T(128)} %param.7) | copy-start | bytes 1540
  119.2 85.0 %all-gather.8.cloned.1.call-start = ((), (), s32[]{:S(2)}) async-start(), calls=%async_computation.4 | async-start | bytes 3145728 | tf_op jit(solution)/shard_map/all_gather | solution.py:95
  153.8 40.3 %copy-start = (f32[512,1024]{1,0:T(8,128)S(1)}, f32[512,1024]{1,0:T(8,128)}, u32[]{:S(2)}) copy-start(f32[512,1024]{1,0:T(8,128)} %reduce-scatter.3.cloned.1.call-done) | copy-start | bytes 6291460
  196.9 54.2 %all-gather.6.cloned.1.call-start = ((), (), s32[]{:S(2)}) async-start(), calls=%async_computation.3 | async-start | bytes 3145728 | tf_op jit(solution)/shard_map/all_gather | solution.py:94
  197.7 85.7 %reduce-scatter.5.cloned.1.call-start = ((), (), s32[]{:S(2)}) async-start(), calls=%async_computation.5 | async-start | bytes 6291456 | tf_op jit(solution)/shard_map/reduce_scatter | solution.py:65
  251.1 13.4 %copy-start.2 = (bf16[8,128,2048]{2,1,0:T(8,128)(2,1)S(1)}, bf16[8,128,2048]{2,1,0:T(8,128)(2,1)}, u32[]{:S(2)}) copy-start(bf16[8,128,2048]{2,1,0:T(8,128)(2,1)} %gather_fusion) | copy-start | bytes 12582916
  261.2 3.2 copy-start.6
  273.9 64.2 %all-gather.10.cloned.1.call-start = ((), (), s32[]{:S(2)}) async-start(), calls=%async_computation.6 | async-start | bytes 3145728 | tf_op jit(solution)/shard_map/all_gather | solution.py:102
  283.4 43.2 %copy-start.1 = (f32[512,1024]{1,0:T(8,128)S(1)}, f32[512,1024]{1,0:T(8,128)}, u32[]{:S(2)}) copy-start(f32[512,1024]{1,0:T(8,128)} %reduce-scatter.5.cloned.1.call-done) | copy-start | bytes 6291460
Sparse Core Ops, SparseCore 0:
  119.3 10.6 reduce-scatter.2
  197.0 7.1 all-gather.7
  205.8 11.8 all-gather.5
  274.1 9.2 reduce-scatter.4
  328.9 9.1 all-gather.9
